TPU v7x, 32 devices: a whole 2x2x4 slice. The times are simulated.
32 devices in a mesh: group: 2 (over y), exp: 4 (over z), tok: 4 (over x, core).
Axes of the slice: x: 2, y: 2, z: 4, core: 2. Of those that a mesh axis runs over, the one named last changes fastest.
Arguments:
- activations: bfloat16 [1024, 2048], P(('group', 'exp'), 'tok'), parts along dimension 0, may hold values from -6 to 6
- expert_ids: int32 [1024, 4], P(('group', 'exp')), parts along dimension 0, may hold values from 0 to 7, all different within a row; in each aligned block of 128 rows (0 to 127, 128 to 255, ...) at most 128 rows name the same one
- gate_values: float32 [1024, 4], P(('group', 'exp')), parts along dimension 0, may hold values from 0.2 to 1
- expert_gate: bfloat16 [8, 2048, 512], P('exp', 'tok'), may hold values from -0.125 to 0.125
- expert_up: bfloat16 [8, 2048, 512], P('exp', 'tok'), may hold values from -0.125 to 0.125
- expert_down: bfloat16 [8, 512, 2048], P('exp', None, 'tok'), may hold values from -0.25 to 0.25
Outputs:
- layer_out: bfloat16 [1024, 2048], P(('group', 'exp'), 'tok'), parts along dimension 0
There are 2 independent parts, one for each index of `group`. A program takes and returns all parts, laid end to end along the dimension named above; an argument that names none is the same for every part. Nothing has to cross between parts.
Inputs may be any that keep to these rules, and one draw needn't show every extreme that they name: `expert_ids`: each row names 4 different experts. Within each aligned block of 128 rows (the tokens of one index of exp) no expert is named by more than 128 rows, and in every draw some expert is named by exactly 128 rows of some block.
All inputs are finite; a program needn't handle non-finite values.
Results may differ from a plain program's by a relative error of at most 0.023.
Values may be sent and summed in bfloat16 or wider, within the bound.
A program may use at most 64 MiB of HBM per device.

v0:
```python
import jax
import jax.numpy as jnp
from jax import lax
from jax.sharding import PartitionSpec as P


def slot_positions(expert_ids, experts_all, capacity):
    flat_ids = expert_ids.reshape(-1)
    one_hot = (flat_ids[:, None] == jnp.arange(experts_all, dtype=jnp.int32)[None, :]).astype(
        jnp.int32
    )
    earlier = jnp.cumsum(one_hot, axis=0) - one_hot
    rank_within = jnp.sum(earlier * one_hot, axis=1)
    return flat_ids * capacity + rank_within


def move_rows(buffer):
    return lax.all_to_all(buffer, "exp", split_axis=0, concat_axis=0, tiled=True)


def shards(activations, expert_ids, gate_values, expert_gate, expert_up, expert_down):
    row_count, feature_cols = activations.shape
    top_count = expert_ids.shape[1]
    local_experts = expert_gate.shape[0]
    groups = lax.axis_size("exp")
    experts_all = local_experts * groups
    capacity = 2 * row_count * top_count // experts_all
    slot_index = slot_positions(expert_ids, experts_all, capacity)
    picked = jnp.repeat(activations, top_count, axis=0)
    outgoing = (
        jnp.zeros((experts_all * capacity, feature_cols), jnp.bfloat16).at[slot_index].set(picked)
    )
    arrived = move_rows(outgoing.reshape(groups, local_experts, capacity, feature_cols))
    gate_part = jnp.einsum(
        "sxcf,xfh->sxch", arrived, expert_gate, preferred_element_type=jnp.float32
    )
    up_part = jnp.einsum("sxcf,xfh->sxch", arrived, expert_up, preferred_element_type=jnp.float32)
    gate_pre, up_pre = (
        lax.psum(gate_part.astype(jnp.bfloat16), "tok").astype(jnp.float32),
        lax.psum(up_part.astype(jnp.bfloat16), "tok").astype(jnp.float32),
    )
    hidden = (jax.nn.silu(gate_pre) * up_pre).astype(jnp.bfloat16)
    results = jnp.einsum(
        "sxch,xhf->sxcf", hidden, expert_down, preferred_element_type=jnp.float32
    ).astype(jnp.bfloat16)
    returned = move_rows(results).reshape(experts_all * capacity, feature_cols)
    fetched = returned[slot_index].astype(jnp.float32).reshape(row_count, top_count, feature_cols)
    combined = jnp.sum(fetched * gate_values[:, :, None], axis=1)
    return combined.astype(jnp.bfloat16)


def solution(mesh):
    placed = (
        P(("group", "exp"), "tok"),
        P(("group", "exp"), None),
        P(("group", "exp"), None),
        P("exp", "tok", None),
        P("exp", "tok", None),
        P("exp", None, "tok"),
    )
    return jax.shard_map(
        shards, mesh=mesh, in_specs=placed, out_specs=P(("group", "exp"), "tok"), check_vma=False
    )
```

profile of v0, /device:TPU:0, one launch (start us, length us, event | category | flops | bytes accessed | tf_op | source)
XLA Modules:
  0.0 144.1 jit_solution(17230130679026216013)
XLA Ops:
  6.5 0.9 copy.15
  7.4 0.1 eq.29
  7.5 0.1 eq.25
  7.6 0.7 broadcast_multiply_fusion
  8.3 1.1 reduce-window.6
  9.5 0.2 slice_reduce_fusion
  9.7 0.1 copy.14
  9.8 0.1 mul.36
  9.9 1.0 broadcast_in_dim.5
  11.0 0.1 reshape.77
  11.1 0.1 fusion.17
  11.2 2.7 %scatter_custom_fusion = bf16[1024,512]{1,0:T(8,128)(2,1)S(1)} fusion(s32[512]{0:T(512)S(1)} %bitcast.35, bf16[512,512]{1,0:T(8,128)(2,1)S(1)} %reshape.77, bf16[]{:T(256)} %constant.6.clone.1), kind=kCustom, calls=%fused_computation.21 | custom fusion | bytes 1048578 | tf_op jit(solution)/shard_map/scatter | solution.py:31
  14.0 31.9 %all_to_all.10 = bf16[4,2,128,512]{3,2,1,0:T(8,128)(2,1)S(1)} all-to-all(bf16[4,2,128,512]{3,2,1,0:T(8,128)(2,1)S(1)} %bitcast.34), channel_id=1, replica_groups=mesh['group'=2,'exp'=4,'tok'=4] {'exp'}, dimensions={0} | all-to-all | bytes 2097152 | tf_op jit(solution)/shard_map/all_to_all | solution.py:18
  45.8 1.7 %fusion.5 = bf16[4,2,128,512]{3,2,0,1:T(8,128)(2,1)} fusion(bf16[2,512,512]{2,1,0:T(8,128)(2,1)S(1)} %copy-done, bf16[4,2,128,512]{3,2,1,0:T(8,128)(2,1)S(1)} %all_to_all.10), kind=kOutput, calls=%fused_computation.12 | convolution fusion | flops 537395200 | bytes 3145728 | tf_op jit(solution)/shard_map/sxcf,xfh->sxch/dot_general | solution.py:34
  47.5 1.7 %fusion.6 = bf16[4,2,128,512]{3,2,0,1:T(8,128)(2,1)} fusion(bf16[2,512,512]{2,1,0:T(8,128)(2,1)S(1)} %copy-done.2, bf16[4,2,128,512]{3,2,1,0:T(8,128)(2,1)S(1)} %all_to_all.10), kind=kOutput, calls=%fused_computation.13 | convolution fusion | flops 537395200 | bytes 3145728 | tf_op jit(solution)/shard_map/sxcf,xfh->sxch/dot_general | solution.py:37
  49.3 50.6 %all-reduce.3.cloned.1.call-done = (bf16[4,2,128,512]{3,2,0,1:T(8,128)(2,1)}, bf16[4,2,128,512]{3,2,0,1:T(8,128)(2,1)}) async-done(((bf16[4,2,128,512]{3,2,0,1:T(8,128)(2,1)}, bf16[4,2,128,512]{3,2,0,1:T(8,128)(2,1)}), (bf16[4,2,128,512]{3,2,0,1:T(8,128)(2,1)}, bf16[4,2,128,512]{3,2,0,1:T(8,128)(2,1)})) %all-reduce.3.cloned.1.call-update) | async-done | bytes 2097168 | tf_op jit(solution)/shard_map/psum | solution.py:40
  99.9 2.3 %fusion.7 = bf16[4,2,128,512]{3,2,0,1:T(8,128)(2,1)S(1)} fusion(bf16[2,512,512]{2,1,0:T(8,128)(2,1)S(1)} %copy-done.3, bf16[4,2,128,512]{3,2,0,1:T(8,128)(2,1)} %get-tuple-element.5, bf16[4,2,128,512]{3,2,0,1:T(8,128)(2,1)} %get-tuple-element.6), kind=kOutput, calls=%fused_computation.14 | convolution fusion | flops 541589504 | bytes 4194304 | tf_op jit(solution)/shard_map/sxch,xhf->sxcf/dot_general | solution.py:43
  102.3 1.1 copy.19
  103.4 4.7 %all-to-all-start.1 = ((bf16[4,2,128,512]{3,2,1,0:T(8,128)(2,1)}), bf16[4,2,128,512]{3,2,1,0:T(8,128)(2,1)S(1)}, u32[]{:S(2)}, u32[]{:S(2)}) async-start(bf16[4,2,128,512]{3,2,1,0:T(8,128)(2,1)} %copy.19), calls=%async_computation.1 | async-start | bytes 2097152 | tf_op jit(solution)/shard_map/all_to_all | solution.py:18
  108.1 0.1 copy.20
  108.2 25.4 %all-to-all-done.1 = bf16[4,2,128,512]{3,2,1,0:T(8,128)(2,1)S(1)} async-done(((bf16[4,2,128,512]{3,2,1,0:T(8,128)(2,1)}), bf16[4,2,128,512]{3,2,1,0:T(8,128)(2,1)S(1)}, u32[]{:S(2)}, u32[]{:S(2)}) %all-to-all-start.1) | async-done | bytes 1048608 | tf_op jit(solution)/shard_map/all_to_all | solution.py:18
  133.6 2.0 %gather_fusion = bf16[512,512]{1,0:T(8,128)(2,1)S(1)} fusion(bf16[1024,512]{1,0:T(8,128)(2,1)S(1)} %bitcast.33, s32[1024]{0:T(1024)S(1)} %pad_clamp_fusion), kind=kCustom, calls=%fused_computation | custom fusion | bytes 1050624 | tf_op jit(solution)/shard_map/gather | solution.py:47
  135.6 0.3 reshape.64
  135.9 1.4 multiply_reduce_fusion
  (15 shorter events, 0.1 us)
Async XLA Ops:
  6.5 39.3 %copy-start = (bf16[2,512,512]{2,1,0:T(8,128)(2,1)S(1)}, bf16[2,512,512]{2,1,0:T(8,128)(2,1)}, u32[]{:S(2)}) copy-start(bf16[2,512,512]{2,1,0:T(8,128)(2,1)} %param.9) | copy-start | bytes 3145732
  6.5 93.4 %all-reduce.3.cloned.1.call-start = ((), (), s32[]{:S(2)}) async-start(), calls=%async_computation.2 | async-start | bytes 4194304 | tf_op jit(solution)/shard_map/psum | solution.py:40
  45.8 1.7 %copy-start.2 = (bf16[2,512,512]{2,1,0:T(8,128)(2,1)S(1)}, bf16[2,512,512]{2,1,0:T(8,128)(2,1)}, u32[]{:S(2)}) copy-start(bf16[2,512,512]{2,1,0:T(8,128)(2,1)} %param.10) | copy-start | bytes 3145732
  49.2 50.7 %copy-start.3 = (bf16[2,512,512]{2,1,0:T(8,128)(2,1)S(1)}, bf16[2,512,512]{2,1,0:T(8,128)(2,1)}, u32[]{:S(2)}) copy-start(bf16[2,512,512]{2,1,0:T(8,128)(2,1)} %param.11) | copy-start | bytes 3145732
  103.4 4.7 %copy-start.1 = (f32[128,4]{0,1:T(4,128)S(1)}, f32[128,4]{0,1:T(4,128)}, u32[]{:S(2)}) copy-start(f32[128,4]{0,1:T(4,128)} %param.8) | copy-start | bytes 6148
  103.4 30.2 %all-to-all-start.1 = ((bf16[4,2,128,512]{3,2,1,0:T(8,128)(2,1)}), bf16[4,2,128,512]{3,2,1,0:T(8,128)(2,1)S(1)}, u32[]{:S(2)}, u32[]{:S(2)}) async-start(bf16[4,2,128,512]{3,2,1,0:T(8,128)(2,1)} %copy.19), calls=%async_computation.1 | async-start | bytes 2097152 | tf_op jit(solution)/shard_map/all_to_all | solution.py:18
Sparse Core Ops, SparseCore 0:
  49.4 50.4 all-reduce.2
where the time goes:
time: 144 us
  waiting for transfers between devices  76 us (53%)
  blocking collectives  31.9 us (22%)
  between operations  13.4 us (9%)
  local copies, waits for them, and re-layouts  8.96 us (6%)
  matrix products  5.73 us (4%)
  starting transfers between devices  4.73 us (3%)
  other arithmetic  3.33 us (2%)
    psum x1, waiting for transfers between devices, shards(): lax.psum(up_part.astype(jnp.bfloat16), 'tok').astype(jnp.float32)  50.6 us
    all_to_all x1, blocking collectives, move_rows(): lax.all_to_all(buffer, 'exp', split_axis=0, concat_axis=0, tiled=True)  31.9 us
    all_to_all x1, waiting for transfers between devices, move_rows(): lax.all_to_all(buffer, 'exp', split_axis=0, concat_axis=0, tiled=True)  25.4 us
    all_to_all x1, starting transfers between devices, move_rows(): lax.all_to_all(buffer, 'exp', split_axis=0, concat_axis=0, tiled=True)  4.73 us
  transfers between devices with their start and end apart: 2, of which 2 were waited for; matrix products, arithmetic and copies ran while one was open for 0% of the time, Pallas kernels for 0%

commit v1 on v0

--- a/solution.py
+++ b/solution.py
@@ -37,7 +37,7 @@
     up_part = jnp.einsum("sxcf,xfh->sxch", arrived, expert_up, preferred_element_type=jnp.float32)
     gate_pre, up_pre = (
         lax.psum(gate_part.astype(jnp.bfloat16), "tok").astype(jnp.float32),
-        lax.psum(up_part.astype(jnp.bfloat16), "tok").astype(jnp.float32),
+        jnp.sum(lax.all_gather(up_part.astype(jnp.bfloat16), "tok"), axis=0).astype(jnp.float32),
     )
     hidden = (jax.nn.silu(gate_pre) * up_pre).astype(jnp.bfloat16)
     results = jnp.einsum(

time: 144 us -> 164 us (1.14)
  waiting for transfers between devices: 76 us -> 92.5 us
  other arithmetic: 3.33 us -> 6.43 us
    all_gather x0 -> x1, waiting for transfers between devices: none -> 31.9 us  [shards(): lax.all_gather(up_part.astype(jnp.bfloat16), 'tok')]
    psum x1, waiting for transfers between devices: 50.6 us -> 35.5 us  [shards(): lax.psum(gate_part.astype(jnp.bfloat16), 'tok').astype(jnp.float32)]
    reduce_sum x0 -> x1, other arithmetic: none -> 3.1 us  [shards(): jnp.sum(lax.all_gather(up_part.astype(jnp.bfloat16), 'tok'), axis=0)]
  transfers between devices with their start and end apart: 2 -> 3, of which waited for: 2 -> 3; matrix products, arithmetic and copies ran while one was open for 0% -> 3% of each run, Pallas kernels for 0% -> 0%
where the time goes in v1:
time: 164 us; the launch traced here: 163 us
  waiting for transfers between devices  92.5 us (56%)
  blocking collectives  31.9 us (19%)
  between operations  13.5 us (8%)
  local copies, waits for them, and re-layouts  8.96 us (5%)
  other arithmetic  6.43 us (4%)
  matrix products  5.49 us (3%)
  starting transfers between devices  4.63 us (3%)
    psum x1, waiting for transfers between devices, shards(): lax.psum(gate_part.astype(jnp.bfloat16), 'tok').astype(jnp.float32)  35.5 us
    all_gather x1, waiting for transfers between devices, shards(): lax.all_gather(up_part.astype(jnp.bfloat16), 'tok')  31.9 us
    all_to_all x1, blocking collectives, move_rows(): lax.all_to_all(buffer, 'exp', split_axis=0, concat_axis=0, tiled=True)  31.9 us
    all_to_all x1, waiting for transfers between devices, move_rows(): lax.all_to_all(buffer, 'exp', split_axis=0, concat_axis=0, tiled=True)  25 us
    all_to_all x1, starting transfers between devices, move_rows(): lax.all_to_all(buffer, 'exp', split_axis=0, concat_axis=0, tiled=True)  4.59 us
  transfers between devices with their start and end apart: 3, of which 3 were waited for; matrix products, arithmetic and copies ran while one was open for 3% of the time, Pallas kernels for 0%

profile of v1, /device:TPU:0, one launch (start us, length us, event | category | flops | bytes accessed | tf_op | source)
XLA Modules:
  0.0 163.4 jit_solution(4618171611394560199)
XLA Ops:
  6.5 0.9 copy.15
  7.5 0.1 eq.25
  7.6 0.7 broadcast_multiply_fusion
  8.3 1.1 reduce-window.6
  9.5 0.2 slice_reduce_fusion
  9.7 0.1 copy.14
  9.8 0.1 mul.36
  9.9 1.0 broadcast_in_dim.5
  11.0 0.1 reshape.77
  11.2 2.7 %scatter_custom_fusion = bf16[1024,512]{1,0:T(8,128)(2,1)S(1)} fusion(s32[512]{0:T(512)S(1)} %bitcast.37, bf16[512,512]{1,0:T(8,128)(2,1)S(1)} %reshape.77, bf16[]{:T(256)} %constant.6.clone.1), kind=kCustom, calls=%fused_computation.21 | custom fusion | bytes 1048578 | tf_op jit(solution)/shard_map/scatter | solution.py:31
  14.0 31.9 %all_to_all.10 = bf16[4,2,128,512]{3,2,1,0:T(8,128)(2,1)S(1)} all-to-all(bf16[4,2,128,512]{3,2,1,0:T(8,128)(2,1)S(1)} %bitcast.36), channel_id=1, replica_groups=mesh['group'=2,'exp'=4,'tok'=4] {'exp'}, dimensions={0} | all-to-all | bytes 2097152 | tf_op jit(solution)/shard_map/all_to_all | solution.py:18
  45.8 1.7 %fusion.6 = bf16[4,2,128,512]{3,2,0,1:T(8,128)(2,1)} fusion(bf16[2,512,512]{2,1,0:T(8,128)(2,1)S(1)} %copy-done, bf16[4,2,128,512]{3,2,1,0:T(8,128)(2,1)S(1)} %all_to_all.10), kind=kOutput, calls=%fused_computation.13 | convolution fusion | flops 537395200 | bytes 3145728 | tf_op jit(solution)/shard_map/sxcf,xfh->sxch/dot_general | solution.py:37
  47.7 1.7 %fusion.5 = bf16[4,2,128,512]{3,2,0,1:T(8,128)(2,1)} fusion(bf16[2,512,512]{2,1,0:T(8,128)(2,1)S(1)} %copy-done.2, bf16[4,2,128,512]{3,2,1,0:T(8,128)(2,1)S(1)} %all_to_all.10), kind=kOutput, calls=%fused_computation.12 | convolution fusion | flops 537395200 | bytes 3145728 | tf_op jit(solution)/shard_map/sxcf,xfh->sxch/dot_general | solution.py:34
  49.4 31.9 %all-gather.3.cloned.1.call-done = bf16[16,2,128,512]{3,2,0,1:T(8,128)(2,1)} async-done(((bf16[4,2,128,512]{3,2,0,1:T(8,128)(2,1)}), bf16[16,2,128,512]{3,2,0,1:T(8,128)(2,1)}) %all-gather.3.cloned.1.call-update) | async-done | bytes 4194320 | tf_op jit(solution)/shard_map/all_gather | solution.py:40
  81.3 3.1 %reduce_sum.34 = bf16[4,2,128,512]{3,2,0,1:T(8,128)(2,1)S(1)} reduce(bf16[4,4,2,128,512]{4,3,1,0,2:T(8,128)(2,1)} %bitcast.35, bf16[]{:T(256)} %constant.6.clone.1), dimensions={0}, to_apply=%region_5.6 | reduce | flops 1572864 | bytes 5242882 | tf_op jit(solution)/shard_map/reduce_sum | solution.py:40
  84.4 35.5 %all-reduce.2.cloned.1.call-done = bf16[4,2,128,512]{3,2,0,1:T(8,128)(2,1)} async-done(((bf16[4,2,128,512]{3,2,0,1:T(8,128)(2,1)}), bf16[4,2,128,512]{3,2,0,1:T(8,128)(2,1)}) %all-reduce.2.cloned.1.call-update) | async-done | bytes 1048592 | tf_op jit(solution)/shard_map/psum | solution.py:39
  120.0 2.0 %fusion.7 = bf16[4,2,128,512]{3,2,0,1:T(8,128)(2,1)S(1)} fusion(bf16[2,512,512]{2,1,0:T(8,128)(2,1)S(1)} %copy-done.3, bf16[4,2,128,512]{3,2,0,1:T(8,128)(2,1)S(1)} %reduce_sum.34, bf16[4,2,128,512]{3,2,0,1:T(8,128)(2,1)} %all-reduce.2.cloned.1.call-done), kind=kOutput, calls=%fused_computation.14 | convolution fusion | flops 541589504 | bytes 4194304 | tf_op jit(solution)/shard_map/sxch,xhf->sxcf/dot_general | solution.py:43
  122.0 1.1 copy.19
  123.1 4.6 %all-to-all-start.1 = ((bf16[4,2,128,512]{3,2,1,0:T(8,128)(2,1)}), bf16[4,2,128,512]{3,2,1,0:T(8,128)(2,1)S(1)}, u32[]{:S(2)}, u32[]{:S(2)}) async-start(bf16[4,2,128,512]{3,2,1,0:T(8,128)(2,1)} %copy.19), calls=%async_computation.1 | async-start | bytes 2097152 | tf_op jit(solution)/shard_map/all_to_all | solution.py:18
  127.7 0.1 copy.20
  127.9 25.0 %all-to-all-done.1 = bf16[4,2,128,512]{3,2,1,0:T(8,128)(2,1)S(1)} async-done(((bf16[4,2,128,512]{3,2,1,0:T(8,128)(2,1)}), bf16[4,2,128,512]{3,2,1,0:T(8,128)(2,1)S(1)}, u32[]{:S(2)}, u32[]{:S(2)}) %all-to-all-start.1) | async-done | bytes 1048608 | tf_op jit(solution)/shard_map/all_to_all | solution.py:18
  152.9 2.0 %gather_fusion = bf16[512,512]{1,0:T(8,128)(2,1)S(1)} fusion(bf16[1024,512]{1,0:T(8,128)(2,1)S(1)} %bitcast.34, s32[1024]{0:T(1024)S(1)} %pad_clamp_fusion), kind=kCustom, calls=%fused_computation | custom fusion | bytes 1050624 | tf_op jit(solution)/shard_map/gather | solution.py:47
  154.9 0.3 reshape.64
  155.2 1.4 multiply_reduce_fusion
  (19 shorter events, 0.3 us)
Async XLA Ops:
  6.5 39.3 %copy-start = (bf16[2,512,512]{2,1,0:T(8,128)(2,1)S(1)}, bf16[2,512,512]{2,1,0:T(8,128)(2,1)}, u32[]{:S(2)}) copy-start(bf16[2,512,512]{2,1,0:T(8,128)(2,1)} %param.10) | copy-start | bytes 3145732
  6.5 74.8 %all-gather.3.cloned.1.call-start = ((), (), s32[]{:S(2)}) async-start(), calls=%async_computation.3 | async-start | bytes 5242880 | tf_op jit(solution)/shard_map/all_gather | solution.py:40
  45.8 1.8 %copy-start.2 = (bf16[2,512,512]{2,1,0:T(8,128)(2,1)S(1)}, bf16[2,512,512]{2,1,0:T(8,128)(2,1)}, u32[]{:S(2)}) copy-start(bf16[2,512,512]{2,1,0:T(8,128)(2,1)} %param.9) | copy-start | bytes 3145732
  47.6 72.4 %all-reduce.2.cloned.1.call-start = ((), (), s32[]{:S(2)}) async-start(), calls=%async_computation.2 | async-start | bytes 2097152 | tf_op jit(solution)/shard_map/psum | solution.py:39
  81.3 38.7 %copy-start.3 = (bf16[2,512,512]{2,1,0:T(8,128)(2,1)S(1)}, bf16[2,512,512]{2,1,0:T(8,128)(2,1)}, u32[]{:S(2)}) copy-start(bf16[2,512,512]{2,1,0:T(8,128)(2,1)} %param.11) | copy-start | bytes 3145732
  122.0 5.7 %copy-start.1 = (f32[128,4]{0,1:T(4,128)S(1)}, f32[128,4]{0,1:T(4,128)}, u32[]{:S(2)}) copy-start(f32[128,4]{0,1:T(4,128)} %param.8) | copy-start | bytes 6148
  123.1 29.7 %all-to-all-start.1 = ((bf16[4,2,128,512]{3,2,1,0:T(8,128)(2,1)}), bf16[4,2,128,512]{3,2,1,0:T(8,128)(2,1)S(1)}, u32[]{:S(2)}, u32[]{:S(2)}) async-start(bf16[4,2,128,512]{3,2,1,0:T(8,128)(2,1)} %copy.19), calls=%async_computation.1 | async-start | bytes 2097152 | tf_op jit(solution)/shard_map/all_to_all | solution.py:18
Sparse Core Ops, SparseCore 0:
  47.7 33.5 all-gather.2
  83.7 36.2 all-reduce.1
